TPU v7x, 32 devices: a whole 2x2x4 slice. The times are simulated.
32 devices in a mesh: ctx: 8 (over y, x, core), fsdp: 4 (over z).
Axes of the slice: x: 2, y: 2, z: 4, core: 2. Of those that a mesh axis runs over, the one named last changes fastest.
Arguments:
- hidden_in: bfloat16 [4, 1024, 768], P('fsdp', 'ctx'), may hold values from -6 to 6
- out_grad: bfloat16 [4, 1024, 768], P('fsdp', 'ctx'), may hold values from -6 to 6
- block_ids: int32 [4, 1024], P('fsdp'), may hold values from 0 to 7, never falling along the last dimension, each value on 1 to 256 neighbouring positions
- clusters: int32 [4, 12, 1024], P('fsdp'), may hold values from 0 to 1023, as said below
- w_query: bfloat16 [768, 768], P('fsdp'), may hold values from -0.21875 to 0.21875
- w_key: bfloat16 [768, 768], P('fsdp'), may hold values from -0.21875 to 0.21875
- w_value: bfloat16 [768, 768], P('fsdp'), may hold values from -0.21875 to 0.21875
- w_out: bfloat16 [768, 768], P('fsdp'), may hold values from -1.25 to 1.25
- b_query: bfloat16 [768], P('fsdp'), may hold values from -3 to 3
- b_value: bfloat16 [768], P('fsdp'), may hold values from -3 to 3
- b_out: bfloat16 [768], P('fsdp'), may hold values from -3 to 3
- ln1_gain: bfloat16 [768], P('fsdp'), may hold values from 0.5 to 1.5
- ln1_bias: bfloat16 [768], P('fsdp'), may hold values from -3 to 3
- w_in: bfloat16 [768, 3072], P('fsdp'), may hold values from -0.21875 to 0.21875
- b_in: bfloat16 [3072], P('fsdp'), may hold values from -3 to 3
- w_down: bfloat16 [3072, 768], P('fsdp'), may hold values from -0.109375 to 0.109375
- b_down: bfloat16 [768], P('fsdp'), may hold values from -3 to 3
- ln2_gain: bfloat16 [768], P('fsdp'), may hold values from 0.5 to 1.5
- ln2_bias: bfloat16 [768], P('fsdp'), may hold values from -3 to 3
Outputs:
- layer_out: bfloat16 [4, 1024, 768], P('fsdp', 'ctx')
- input_grad: bfloat16 [4, 1024, 768], P('fsdp', 'ctx')
- grad_w_query: float32 [768, 768], P('fsdp')
- grad_w_key: float32 [768, 768], P('fsdp')
- grad_w_value: float32 [768, 768], P('fsdp')
- grad_w_out: float32 [768, 768], P('fsdp')
- grad_b_query: float32 [768], P('fsdp')
- grad_b_value: float32 [768], P('fsdp')
- grad_b_out: float32 [768], P('fsdp')
- grad_ln1_gain: float32 [768], P('fsdp')
- grad_ln1_bias: float32 [768], P('fsdp')
- grad_w_in: float32 [768, 3072], P('fsdp')
- grad_b_in: float32 [3072], P('fsdp')
- grad_w_down: float32 [3072, 768], P('fsdp')
- grad_b_down: float32 [768], P('fsdp')
- grad_ln2_gain: float32 [768], P('fsdp')
- grad_ln2_bias: float32 [768], P('fsdp')
Inputs may be any that keep to these rules, and one draw needn't show every extreme that they name: `clusters`: each head's row is an order of all 1024 stored rows of its sequence; every cluster (128 consecutive entries) holds exactly 16 stored rows of each aligned range of 128 stored rows. `block_ids`: never falls along the positions; each block holds 1 to 256 positions.
All inputs are finite; a program needn't handle non-finite values.
Results may differ from a plain program's by a relative error of at most 0.022.
Values may be sent and summed in bfloat16 or wider, within the bound.
No kernel may reach another device: no remote copies, remote signals or barrier semaphores. Data moves between devices by JAX's collectives and lax.ppermute only.
A program may use at most 192 MiB of HBM per device.

v0:
```python
import jax
import jax.numpy as jnp
from jax import lax
from jax.sharding import PartitionSpec as P

H = 12
DH = 64
CLUSTER = 128
EPSILON = 1e-12
FLOOR = -1e30


def layer_norm(values, gain, shift):
    centre = values - jnp.mean(values, axis=-1, keepdims=True)
    spread = jnp.mean(centre * centre, axis=-1, keepdims=True)
    return centre * lax.rsqrt(spread + EPSILON) * gain + shift


def exact_gelu(values):
    return jax.nn.gelu(values, approximate=False)


def positions(length, per_device, parts):
    stored = jnp.arange(length, dtype=jnp.int32)
    device = stored // per_device
    within = stored % per_device
    half = per_device // 2
    return jnp.where(
        within < half, device * half + within, (2 * parts - 1 - device) * half + within - half
    )


def contract(left, right):
    return lax.dot_general(
        left, right, (((0,), (0,)), ((), ())), preferred_element_type=jnp.float32
    )


def back_product(grad, weight):
    return lax.dot_general(
        grad, weight, (((1,), (1,)), ((), ())), preferred_element_type=jnp.float32
    )


def column_sum(values):
    return jnp.sum(values.astype(jnp.float32), axis=0)


def per_head_rows(rows, index):
    split = rows.reshape(rows.shape[0], H, DH)
    return jnp.take_along_axis(split, index.T[:, :, None], axis=0)


def cluster_tables(order, device, per_device, parts):
    heads, length = order.shape
    groups = length // CLUSTER
    members = CLUSTER // parts
    mine = (order // per_device == device).astype(jnp.int32)
    rank = jnp.cumsum(mine.reshape(heads, groups, CLUSTER), axis=-1).reshape(heads, length) - 1
    entry = jnp.arange(length, dtype=jnp.int32)[None, :]
    slot = jnp.where(mine == 1, entry // CLUSTER * members + rank, per_device)
    head_index = jnp.arange(heads, dtype=jnp.int32)[:, None]
    picked = (
        jnp.zeros((heads, per_device), jnp.int32)
        .at[head_index, slot]
        .set(order - device * per_device, mode="drop")
    )
    counter = jnp.broadcast_to(
        jnp.arange(per_device, dtype=jnp.int32)[None, :], (heads, per_device)
    )
    placed = jnp.zeros((heads, per_device), jnp.int32).at[head_index, picked].set(counter)
    inverse = (
        jnp.zeros((heads, length), jnp.int32)
        .at[head_index, order]
        .set(jnp.broadcast_to(jnp.arange(length, dtype=jnp.int32)[None, :], (heads, length)))
    )
    return (picked, placed, inverse)


def score_blocks(query, key_rows, query_blocks, key_blocks, scale):
    scores = (
        jnp.einsum("cqhd,ckhd->hcqk", query, key_rows, preferred_element_type=jnp.float32) * scale
    )
    allowed = key_blocks[:, :, None, :] <= query_blocks[:, :, :, None]
    return (scores, allowed)


def attend(query, key_rows, value_rows, query_blocks, key_blocks, scale):
    scores, allowed = score_blocks(query, key_rows, query_blocks, key_blocks, scale)
    masked = jnp.where(allowed, scores, FLOOR)
    top = jnp.max(masked, axis=-1, keepdims=True)
    weights = jnp.where(allowed, jnp.exp(masked - top), 0.0)
    total = jnp.sum(weights, axis=-1, keepdims=True)
    probs = (weights / total).astype(jnp.bfloat16)
    mixed = jnp.einsum("hcqk,ckhd->cqhd", probs, value_rows, preferred_element_type=jnp.float32)
    return (mixed.astype(jnp.bfloat16), top + jnp.log(total))


def attend_back(query, key_rows, value_rows, query_blocks, key_blocks, logsum, d_mixed, scale):
    scores, allowed = score_blocks(query, key_rows, query_blocks, key_blocks, scale)
    probs = jnp.where(allowed, jnp.exp(jnp.where(allowed, scores, FLOOR) - logsum), 0.0)
    rounded = probs.astype(jnp.bfloat16)
    d_probs = jnp.einsum("cqhd,ckhd->hcqk", d_mixed, value_rows, preferred_element_type=jnp.float32)
    centred = jnp.sum(probs * d_probs, axis=-1, keepdims=True)
    d_scores = (probs * (d_probs - centred)).astype(jnp.bfloat16)
    d_query = (
        jnp.einsum("hcqk,ckhd->cqhd", d_scores, key_rows, preferred_element_type=jnp.float32)
        * scale
    )
    d_key = (
        jnp.einsum("hcqk,cqhd->ckhd", d_scores, query, preferred_element_type=jnp.float32) * scale
    )
    d_value = jnp.einsum("hcqk,cqhd->ckhd", rounded, d_mixed, preferred_element_type=jnp.float32)
    return (d_query, d_key, d_value)


def body(
    hidden_in,
    out_grad,
    block_ids,
    clusters,
    w_query,
    w_key,
    w_value,
    w_out,
    b_query,
    b_value,
    b_out,
    ln1_gain,
    ln1_bias,
    w_in,
    b_in,
    w_down,
    b_down,
    ln2_gain,
    ln2_bias,
):
    parts = lax.axis_size("ctx")
    device = lax.axis_index("ctx")
    sequences, per_device, width = hidden_in.shape
    length = per_device * parts
    members = CLUSTER // parts
    groups = length // CLUSTER
    scale = DH ** (-0.5)
    (
        full_query,
        full_key,
        full_value,
        full_out,
        bias_query,
        bias_value,
        bias_out,
        gain_one,
        shift_one,
    ) = (
        lax.all_gather(w_query, "fsdp", axis=0, tiled=True),
        lax.all_gather(w_key, "fsdp", axis=0, tiled=True),
        lax.all_gather(w_value, "fsdp", axis=0, tiled=True),
        lax.all_gather(w_out, "fsdp", axis=0, tiled=True),
        lax.all_gather(b_query, "fsdp", axis=0, tiled=True),
        lax.all_gather(b_value, "fsdp", axis=0, tiled=True),
        lax.all_gather(b_out, "fsdp", axis=0, tiled=True),
        lax.all_gather(ln1_gain, "fsdp", axis=0, tiled=True),
        lax.all_gather(ln1_bias, "fsdp", axis=0, tiled=True),
    )
    full_in, full_down, bias_in, bias_down, gain_two, shift_two = (
        lax.all_gather(w_in, "fsdp", axis=0, tiled=True),
        lax.all_gather(w_down, "fsdp", axis=0, tiled=True),
        lax.all_gather(b_in, "fsdp", axis=0, tiled=True),
        lax.all_gather(b_down, "fsdp", axis=0, tiled=True),
        lax.all_gather(ln2_gain, "fsdp", axis=0, tiled=True),
        lax.all_gather(ln2_bias, "fsdp", axis=0, tiled=True),
    )
    hidden = hidden_in.reshape(sequences * per_device, width)
    query_rows = (
        jnp.dot(hidden, full_query, preferred_element_type=jnp.float32) + bias_query
    ).astype(jnp.bfloat16)
    key_rows = jnp.dot(hidden, full_key, preferred_element_type=jnp.float32).astype(jnp.bfloat16)
    value_rows = (
        jnp.dot(hidden, full_value, preferred_element_type=jnp.float32) + bias_value
    ).astype(jnp.bfloat16)
    place = positions(length, per_device, parts)
    index = 0
    order = clusters[index]
    stored_blocks = block_ids[index][place]
    picked, placed, inverse = cluster_tables(order, device, per_device, parts)
    q_local = per_head_rows(query_rows, picked).reshape(groups, members, H, DH)
    query_blocks = stored_blocks[device * per_device + picked].reshape(H, groups, members)
    key_all = lax.all_gather(key_rows, "ctx", axis=0, tiled=True)
    value_all = lax.all_gather(value_rows, "ctx", axis=0, tiled=True)
    key_cluster = per_head_rows(key_all, order).reshape(groups, CLUSTER, H, DH)
    value_cluster = per_head_rows(value_all, order).reshape(groups, CLUSTER, H, DH)
    key_blocks = stored_blocks[order].reshape(H, groups, CLUSTER)
    mixed, logsum = attend(q_local, key_cluster, value_cluster, query_blocks, key_blocks, scale)
    contexts = per_head_rows(mixed.reshape(per_device, width), placed).reshape(per_device, width)
    kept = [
        (
            q_local,
            key_cluster,
            value_cluster,
            query_blocks,
            key_blocks,
            logsum,
            picked,
            placed,
            inverse,
        )
    ]
    attended = jnp.dot(contexts, full_out, preferred_element_type=jnp.float32) + bias_out
    first_sum = hidden.astype(jnp.float32) + attended
    first, first_pull = jax.vjp(
        layer_norm, first_sum, gain_one.astype(jnp.float32), shift_one.astype(jnp.float32)
    )
    first_low = first.astype(jnp.bfloat16)
    inner = jnp.dot(first_low, full_in, preferred_element_type=jnp.float32) + bias_in
    active_full, gelu_pull = jax.vjp(exact_gelu, inner)
    active = active_full.astype(jnp.bfloat16)
    second_sum = first + jnp.dot(active, full_down, preferred_element_type=jnp.float32) + bias_down
    second, second_pull = jax.vjp(
        layer_norm, second_sum, gain_two.astype(jnp.float32), shift_two.astype(jnp.float32)
    )
    layer_out = second.astype(jnp.bfloat16).reshape(sequences, per_device, width)
    d_out = out_grad.reshape(sequences * per_device, width).astype(jnp.float32)
    d_second, g_gain_two, g_shift_two = second_pull(d_out)
    d_branch = d_second.astype(jnp.bfloat16)
    g_w_down = contract(active, d_branch)
    g_b_down = column_sum(d_branch)
    d_active = back_product(d_branch, full_down)
    d_inner = gelu_pull(d_active)[0].astype(jnp.bfloat16)
    g_w_in = contract(first_low, d_inner)
    g_b_in = column_sum(d_inner)
    d_first = d_second + back_product(d_inner, full_in)
    d_sum, g_gain_one, g_shift_one = first_pull(d_first)
    d_attended = d_sum.astype(jnp.bfloat16)
    g_w_out = contract(contexts, d_attended)
    g_b_out = column_sum(d_attended)
    d_context = back_product(d_attended, full_out).astype(jnp.bfloat16)
    index = 0
    q_kept, k_kept, v_kept, blocks_q, blocks_k, logsum, picked, placed, inverse = kept[index]
    d_cluster = per_head_rows(d_context, picked).reshape(groups, members, H, DH)
    d_query, d_key, d_value = attend_back(
        q_kept, k_kept, v_kept, blocks_q, blocks_k, logsum, d_cluster, scale
    )
    key_full = per_head_rows(d_key.reshape(length, width), inverse).reshape(length, width)
    value_full = per_head_rows(d_value.reshape(length, width), inverse).reshape(length, width)
    key_part = lax.psum_scatter(
        key_full.astype(jnp.bfloat16), "ctx", scatter_dimension=0, tiled=True
    )
    value_part = lax.psum_scatter(
        value_full.astype(jnp.bfloat16), "ctx", scatter_dimension=0, tiled=True
    )
    query_local = d_query.astype(jnp.bfloat16).reshape(per_device, width)
    query_grads = per_head_rows(query_local, placed).reshape(per_device, width)
    g_w_query = contract(hidden, query_grads)
    g_b_query = column_sum(query_grads)
    g_w_key = contract(hidden, key_part)
    g_w_value = contract(hidden, value_part)
    g_b_value = column_sum(value_part)
    input_total = (
        d_sum
        + back_product(query_grads, full_query)
        + back_product(key_part, full_key)
        + back_product(value_part, full_value)
    )
    input_grad = input_total.astype(jnp.bfloat16).reshape(sequences, per_device, width)
    shares = (
        lax.psum_scatter(
            g_w_query.astype(jnp.bfloat16), "fsdp", scatter_dimension=0, tiled=True
        ).astype(jnp.float32),
        lax.psum_scatter(
            g_w_key.astype(jnp.bfloat16), "fsdp", scatter_dimension=0, tiled=True
        ).astype(jnp.float32),
        lax.psum_scatter(
            g_w_value.astype(jnp.bfloat16), "fsdp", scatter_dimension=0, tiled=True
        ).astype(jnp.float32),
        lax.psum_scatter(
            g_w_out.astype(jnp.bfloat16), "fsdp", scatter_dimension=0, tiled=True
        ).astype(jnp.float32),
        lax.psum_scatter(
            g_b_query.astype(jnp.bfloat16), "fsdp", scatter_dimension=0, tiled=True
        ).astype(jnp.float32),
        lax.psum_scatter(
            g_b_value.astype(jnp.bfloat16), "fsdp", scatter_dimension=0, tiled=True
        ).astype(jnp.float32),
        lax.psum_scatter(
            g_b_out.astype(jnp.bfloat16), "fsdp", scatter_dimension=0, tiled=True
        ).astype(jnp.float32),
        lax.psum_scatter(
            g_gain_one.astype(jnp.bfloat16), "fsdp", scatter_dimension=0, tiled=True
        ).astype(jnp.float32),
        lax.psum_scatter(
            g_shift_one.astype(jnp.bfloat16), "fsdp", scatter_dimension=0, tiled=True
        ).astype(jnp.float32),
        lax.psum_scatter(
            g_w_in.astype(jnp.bfloat16), "fsdp", scatter_dimension=0, tiled=True
        ).astype(jnp.float32),
        lax.psum_scatter(
            g_b_in.astype(jnp.bfloat16), "fsdp", scatter_dimension=0, tiled=True
        ).astype(jnp.float32),
        lax.psum_scatter(
            g_w_down.astype(jnp.bfloat16), "fsdp", scatter_dimension=0, tiled=True
        ).astype(jnp.float32),
        lax.psum_scatter(
            g_b_down.astype(jnp.bfloat16), "fsdp", scatter_dimension=0, tiled=True
        ).astype(jnp.float32),
        lax.psum_scatter(
            g_gain_two.astype(jnp.bfloat16), "fsdp", scatter_dimension=0, tiled=True
        ).astype(jnp.float32),
        lax.psum_scatter(
            g_shift_two.astype(jnp.bfloat16), "fsdp", scatter_dimension=0, tiled=True
        ).astype(jnp.float32),
    )
    totals = (
        lax.psum(shares[0].astype(jnp.bfloat16), "ctx").astype(jnp.float32),
        lax.psum(shares[1].astype(jnp.bfloat16), "ctx").astype(jnp.float32),
        lax.psum(shares[2].astype(jnp.bfloat16), "ctx").astype(jnp.float32),
        lax.psum(shares[3].astype(jnp.bfloat16), "ctx").astype(jnp.float32),
        lax.psum(shares[4].astype(jnp.bfloat16), "ctx").astype(jnp.float32),
        lax.psum(shares[5].astype(jnp.bfloat16), "ctx").astype(jnp.float32),
        lax.psum(shares[6].astype(jnp.bfloat16), "ctx").astype(jnp.float32),
        lax.psum(shares[7].astype(jnp.bfloat16), "ctx").astype(jnp.float32),
        lax.psum(shares[8].astype(jnp.bfloat16), "ctx").astype(jnp.float32),
        lax.psum(shares[9].astype(jnp.bfloat16), "ctx").astype(jnp.float32),
        lax.psum(shares[10].astype(jnp.bfloat16), "ctx").astype(jnp.float32),
        lax.psum(shares[11].astype(jnp.bfloat16), "ctx").astype(jnp.float32),
        lax.psum(shares[12].astype(jnp.bfloat16), "ctx").astype(jnp.float32),
        lax.psum(shares[13].astype(jnp.bfloat16), "ctx").astype(jnp.float32),
        lax.psum(shares[14].astype(jnp.bfloat16), "ctx").astype(jnp.float32),
    )
    return (
        layer_out,
        input_grad,
        totals[0],
        totals[1],
        totals[2],
        totals[3],
        totals[4],
        totals[5],
        totals[6],
        totals[7],
        totals[8],
        totals[9],
        totals[10],
        totals[11],
        totals[12],
        totals[13],
        totals[14],
    )


def solution(mesh):
    in_specs = (
        P("fsdp", "ctx", None),
        P("fsdp", "ctx", None),
        P("fsdp", None),
        P("fsdp", None, None),
        P("fsdp", None),
        P("fsdp", None),
        P("fsdp", None),
        P("fsdp", None),
        P("fsdp"),
        P("fsdp"),
        P("fsdp"),
        P("fsdp"),
        P("fsdp"),
        P("fsdp", None),
        P("fsdp"),
        P("fsdp", None),
        P("fsdp"),
        P("fsdp"),
        P("fsdp"),
    )
    out_specs = (
        P("fsdp", "ctx", None),
        P("fsdp", "ctx", None),
        P("fsdp", None),
        P("fsdp", None),
        P("fsdp", None),
        P("fsdp", None),
        P("fsdp"),
        P("fsdp"),
        P("fsdp"),
        P("fsdp"),
        P("fsdp"),
        P("fsdp", None),
        P("fsdp"),
        P("fsdp", None),
        P("fsdp"),
        P("fsdp"),
        P("fsdp"),
    )
    return jax.shard_map(body, mesh=mesh, in_specs=in_specs, out_specs=out_specs, check_vma=False)
```

profile of v0, /device:TPU:0, one launch (start us, length us, event | category | flops | bytes accessed | tf_op | source)
XLA Modules:
  0.0 1361.8 jit_solution(14786672146078861802)
XLA Ops:
  17.3 21.1 %all-reduce.20 = (bf16[768]{0:T(1024)(128)(2,1)S(1)}, bf16[768]{0:T(1024)(128)(2,1)S(1)}, bf16[768]{0:T(1024)(128)(2,1)S(1)}, bf16[768]{0:T(1024)(128)(2,1)S(1)}...) all-reduce(bf16[768]{0:T(1024)(128)(2,1)S(1)} %dynamic-update-slice, ...), channel_id=1, replica_groups=mesh['ctx'=8,'fsdp'=4] {'fsdp'}, use_global_device_ids=true, to_apply=%add | all-reduce | flops 5376 | bytes 21504
  38.4 4.9 all-gather.10.cloned.1.call-done
  45.8 28.7 %all-gather.16.cloned.1.call-done = bf16[768,768]{1,0:T(8,128)(2,1)} async-done(((bf16[192,768]{1,0:T(8,128)(2,1)}), bf16[768,768]{1,0:T(8,128)(2,1)}) %all-gather.16.cloned.1.call-update) | async-done | bytes 1179664 | tf_op jit(solution)/shard_map/all_gather | solution.py:157
  79.0 3.4 reduce_window_sum.11
  83.7 45.4 %scatter_custom_fusion = s32[1536]{0:T(1024)S(1)} fusion(s32[12288]{0:T(1024)S(1)} %reshape.537, s32[12288]{0:T(1024)S(1)} %reshape.539, s32[]{:T(128)} %constant.79.clone.1), kind=kCustom, calls=%fused_computation.202 | custom fusion | bytes 6148
  129.6 4.5 gather_fusion
  134.2 5.9 gather_fusion.2
  142.3 49.1 %gather_fusion.1 = s32[12288]{0:T(1024)S(1)} fusion(s32[1024]{0:T(1024)S(1)} %gather_fusion, s32[12288]{0:T(1024)S(1)} %broadcast_clamp_fusion), kind=kCustom, calls=%fused_computation.9 | custom fusion | bytes 147456 | tf_op jit(solution)/shard_map/gather | solution.py:193
  191.5 6.2 scatter_custom_fusion.1
  198.2 13.3 all-gather
  212.7 45.6 %scatter_custom_fusion.2 = s32[12288]{0:T(1024)S(1)} fusion(s32[12288]{0:T(1024)S(1)} %reshape.549, s32[12288]{0:T(1024)S(1)} %reshape.551, s32[]{:T(128)} %constant.79.clone.1), kind=kCustom, calls=%fused_computation.165 | custom fusion | bytes 49156
  261.6 8.5 gather_fusion.4
  274.1 3.1 copy.214
  277.1 119.4 %gather_fusion.3 = bf16[12288,64]{1,0:T(8,128)(2,1)} fusion(bf16[1024,12,64]{2,0,1:T(8,128)(2,1)S(1)} %copy.214, s32[12288]{0:T(1024)S(1)} %reshape.603), kind=kCustom, calls=%fused_computation.clone | custom fusion | bytes 3244032 | tf_op jit(solution)/shard_map/jit(take_along_axis)/gather | solution.py:51
  396.5 6.6 reshape.606
  405.7 3.1 copy.224
  408.7 119.3 %gather_fusion.5 = bf16[12288,64]{1,0:T(8,128)(2,1)} fusion(bf16[1024,12,64]{2,0,1:T(8,128)(2,1)S(1)} %copy.224, s32[12288]{0:T(1024)S(1)} %reshape.603), kind=kCustom, calls=%fused_computation.3.clone | custom fusion | bytes 3244032 | tf_op jit(solution)/shard_map/jit(take_along_axis)/gather | solution.py:51
  528.1 6.6 reshape.614
  534.7 10.9 broadcast_select_fusion
  550.8 8.5 gather_fusion.6
  562.3 8.6 multiply_convert_fusion
  571.0 3.6 fusion.105
  584.8 8.5 gather_fusion.7
  596.3 3.1 copy.268
  599.4 119.4 %gather_fusion.10 = bf16[12288,64]{1,0:T(8,128)(2,1)} fusion(bf16[1024,12,64]{2,0,1:T(8,128)(2,1)S(1)} %bitcast.190, s32[12288]{0:T(1024)S(1)} %reshape.627), kind=kCustom, calls=%fused_computation.7.clone | custom fusion | bytes 3244032 | tf_op jit(solution)/shard_map/jit(take_along_axis)/gather | solution.py:51
  718.8 6.6 reshape.634
  725.4 5.7 copy.255
  731.1 4.0 fusion.1
  735.1 8.4 fusion.32
  746.0 3.1 copy.266
  749.1 119.4 %gather_fusion.9 = bf16[12288,64]{1,0:T(8,128)(2,1)} fusion(bf16[1024,12,64]{2,0,1:T(8,128)(2,1)S(1)} %bitcast.189, s32[12288]{0:T(1024)S(1)} %reshape.627), kind=kCustom, calls=%fused_computation.2.clone | custom fusion | bytes 3244032 | tf_op jit(solution)/shard_map/jit(take_along_axis)/gather | solution.py:51
  868.5 6.6 reshape.630
  875.0 5.3 copy.249
  887.3 3.1 fusion.36
  890.5 8.5 gather_fusion.8
  901.9 20.9 %reduce-scatter.25.cloned.1.call-done = bf16[128,768]{1,0:T(8,128)(2,1)} async-done(((bf16[1024,768]{1,0:T(8,128)(2,1)}), bf16[128,768]{1,0:T(8,128)(2,1)}) %reduce-scatter.25.cloned.1.call-update) | async-done | bytes 196624
  925.7 39.2 %reduce-scatter.27.cloned.1.call-done = bf16[128,768]{1,0:T(8,128)(2,1)} async-done(((bf16[1024,768]{1,0:T(8,128)(2,1)}), bf16[128,768]{1,0:T(8,128)(2,1)}) %reduce-scatter.27.cloned.1.call-update) | async-done | bytes 196624
  969.7 3.7 convolution_convert_fusion.1
  974.5 3.6 convolution_convert_fusion
  978.2 18.2 %reduce-scatter.29.cloned.1.call-done = bf16[192,768]{1,0:T(8,128)(2,1)} async-done(((bf16[768,768]{1,0:T(8,128)(2,1)}), bf16[192,768]{1,0:T(8,128)(2,1)}) %reduce-scatter.29.cloned.1.call-update) | async-done | bytes 294928
  998.3 28.8 %reduce-scatter.31.cloned.1.call-done = bf16[192,768]{1,0:T(8,128)(2,1)} async-done(((bf16[768,768]{1,0:T(8,128)(2,1)}), bf16[192,768]{1,0:T(8,128)(2,1)}) %reduce-scatter.31.cloned.1.call-update) | async-done | bytes 294928
  1029.0 28.9 %reduce-scatter.33.cloned.1.call-done = bf16[192,768]{1,0:T(8,128)(2,1)} async-done(((bf16[768,768]{1,0:T(8,128)(2,1)}), bf16[192,768]{1,0:T(8,128)(2,1)}) %reduce-scatter.33.cloned.1.call-update) | async-done | bytes 294928
  1059.8 28.2 %reduce-scatter.19.cloned.1.call-done = bf16[192,768]{1,0:T(8,128)(2,1)} async-done(((bf16[768,768]{1,0:T(8,128)(2,1)}), bf16[192,768]{1,0:T(8,128)(2,1)}) %reduce-scatter.19.cloned.1.call-update) | async-done | bytes 294928 | tf_op jit(solution)/shard_map/reduce_scatter | solution.py:276
  1088.1 86.1 %reduce-scatter.21.cloned.1.call-done = bf16[192,3072]{1,0:T(8,128)(2,1)} async-done(((bf16[768,3072]{1,0:T(8,128)(2,1)}), bf16[192,3072]{1,0:T(8,128)(2,1)}) %reduce-scatter.21.cloned.1.call-update) | async-done | bytes 1179664 | tf_op jit(solution)/shard_map/reduce_scatter | solution.py:294
  1174.2 88.0 %reduce-scatter.23.cloned.1.call-done = bf16[768,768]{1,0:T(8,128)(2,1)} async-done(((bf16[3072,768]{1,0:T(8,128)(2,1)}), bf16[768,768]{1,0:T(8,128)(2,1)}) %reduce-scatter.23.cloned.1.call-update) | async-done | bytes 1179664 | tf_op jit(solution)/shard_map/reduce_scatter | solution.py:300
  1268.1 18.3 %all-reduce.19 = (bf16[768]{0:T(1024)(128)(2,1)S(1)}, bf16[768]{0:T(1024)(128)(2,1)S(1)}, bf16[768]{0:T(1024)(128)(2,1)S(1)}, bf16[768]{0:T(1024)(128)(2,1)S(1)}...) all-reduce(bf16[768]{0:T(1024)(128)(2,1)S(1)} %dynamic-update-slice, ...), channel_id=1, replica_groups=mesh['ctx'=8,'fsdp'=4] {'fsdp'}, use_global_device_ids=true, to_apply=%add.7 | all-reduce | flops 9984 | bytes 39936
  1287.1 12.0 all-reduce.17
  1307.9 38.7 %all-reduce.23.cloned.1.call-done = (bf16[192,768]{0,1:T(8,128)(2,1)}, bf16[192,768]{0,1:T(8,128)(2,1)}, bf16[192,768]{0,1:T(8,128)(2,1)}, bf16[192,768]{1,0:T(8...) async-done(((bf16[192,768]{0,1:T(8,128)(2,1)}, bf16[192,768]{0,1:T(8,128)(2,1)}, bf16[192,768]{0,1:T(8,128)(2,1)}, bf16[192,768]{1,0:T(8,128)(2,1)}, ...) | async-done | bytes 3538960 | tf_op jit(solution)/shard_map/psum | solution.py:314
  (357 shorter events, 102.0 us)
Async XLA Ops:
  7.2 122.4 %copy-start = (s32[1,1024]{1,0:T(1,128)S(1)}, s32[1,1024]{1,0:T(1,128)}, u32[]{:S(2)}) copy-start(s32[1,1024]{1,0:T(1,128)} %param.27) | copy-start | bytes 12292
  7.2 67.3 %copy-start.8 = (bf16[1,128,768]{2,1,0:T(8,128)(2,1)S(1)}, bf16[1,128,768]{2,1,0:T(8,128)(2,1)}, u32[]{:S(2)}) copy-start(bf16[1,128,768]{2,1,0:T(8,128)(2,1)} %param.25) | copy-start | bytes 589828
  7.2 36.1 %all-gather.10.cloned.1.call-start = ((), (), s32[]{:S(2)}) async-start(), calls=%async_computation.8 | async-start | bytes 1474560 | tf_op jit(solution)/shard_map/all_gather | solution.py:158
  8.0 66.5 %all-gather.16.cloned.1.call-start = ((), (), s32[]{:S(2)}) async-start(), calls=%async_computation.11 | async-start | bytes 1474560 | tf_op jit(solution)/shard_map/all_gather | solution.py:157
  8.7 250.9 %all-gather.14.cloned.1.call-start = ((), (), s32[]{:S(2)}) async-start(), calls=%async_computation.10 | async-start | bytes 1474560 | tf_op jit(solution)/shard_map/all_gather | solution.py:156
  9.4 262.0 %all-gather.12.cloned.1.call-start = ((), (), s32[]{:S(2)}) async-start(), calls=%async_computation.9 | async-start | bytes 1769472 | tf_op jit(solution)/shard_map/all_gather | solution.py:190
  45.8 357.4 %all-gather.18.cloned.1.call-start = ((), (), s32[]{:S(2)}) async-start(), calls=%async_computation.12 | async-start | bytes 1769472 | tf_op jit(solution)/shard_map/all_gather | solution.py:189
  76.8 6.0 copy-start.63
  76.8 6.0 copy-start.68
  76.8 483.4 %all-gather.20.cloned.1.call-start = ((), (), s32[]{:S(2)}) async-start(), calls=%async_computation.13 | async-start | bytes 1474560 | tf_op jit(solution)/shard_map/all_gather | solution.py:159
  77.4 5.8 copy-start.64
  77.4 5.8 copy-start.67
  77.4 484.8 %all-gather.22.cloned.1.call-start = ((), (), s32[]{:S(2)}) async-start(), calls=%async_computation.14 | async-start | bytes 5898240 | tf_op jit(solution)/shard_map/all_gather | solution.py:167
  78.2 492.7 %all-gather.24.cloned.1.call-start = ((), (), s32[]{:S(2)}) async-start(), calls=%async_computation.15 | async-start | bytes 5898240 | tf_op jit(solution)/shard_map/all_gather | solution.py:168
  78.9 843.9 %reduce-scatter.25.cloned.1.call-start = ((), (), s32[]{:S(2)}) async-start(), calls=%async_computation.19 | async-start | bytes 1769472
  142.3 55.9 %copy-start.65 = (bf16[768]{0:T(1024)(128)(2,1)S(1)}, bf16[768]{0:T(1024)(128)(2,1)}, u32[]{:S(2)}) copy-start(bf16[768]{0:T(1024)(128)(2,1)} %param.39) | copy-start | bytes 4612
  528.1 6.6 copy-start.40
  534.7 11.0 copy-start.30
  534.7 11.0 copy-start.36
  545.7 5.1 copy-start.3
  562.0 20.4 %copy-start.4 = (f32[128,768]{1,0:T(8,128)}, f32[128,768]{1,0:T(8,128)S(1)}, u32[]{:S(2)}) copy-start(f32[128,768]{1,0:T(8,128)S(1)} %get-tuple-element.175) | copy-start | bytes 1179652
  562.2 20.2 %copy-start.49 = (f32[128]{0:T(128)}, f32[128]{0:T(128)S(1)}, u32[]{:S(2)}) copy-start(f32[128]{0:T(128)S(1)} %fusion.91) | copy-start | bytes 1540
  562.3 8.6 copy-start.48
  570.9 5.7 slice-start.2
  570.9 5.6 slice-start.3
  571.0 5.6 copy-start.70
  574.6 4.4 copy-start.58
  725.4 5.7 copy-start.31
  735.1 9.1 copy-start.18
  875.0 5.3 copy-start.47
  884.7 80.3 %reduce-scatter.27.cloned.1.call-start = ((), (), s32[]{:S(2)}) async-start(), calls=%async_computation.20 | async-start | bytes 1769472
  886.3 110.1 %reduce-scatter.29.cloned.1.call-start = ((), (), s32[]{:S(2)}) async-start(), calls=%async_computation.21 | async-start | bytes 1474560
  901.8 125.3 %reduce-scatter.31.cloned.1.call-start = ((), (), s32[]{:S(2)}) async-start(), calls=%async_computation.22 | async-start | bytes 1474560
  925.7 132.3 %reduce-scatter.33.cloned.1.call-start = ((), (), s32[]{:S(2)}) async-start(), calls=%async_computation.23 | async-start | bytes 1474560
  967.9 120.2 %reduce-scatter.19.cloned.1.call-start = ((), (), s32[]{:S(2)}) async-start(), calls=%async_computation.16 | async-start | bytes 1474560 | tf_op jit(solution)/shard_map/reduce_scatter | solution.py:276
  969.5 204.7 %reduce-scatter.21.cloned.1.call-start = ((), (), s32[]{:S(2)}) async-start(), calls=%async_computation.17 | async-start | bytes 5898240 | tf_op jit(solution)/shard_map/reduce_scatter | solution.py:294
  973.4 288.8 %reduce-scatter.23.cloned.1.call-start = ((), (), s32[]{:S(2)}) async-start(), calls=%async_computation.18 | async-start | bytes 5898240 | tf_op jit(solution)/shard_map/reduce_scatter | solution.py:300
  978.2 368.5 %all-reduce.23.cloned.1.call-start = ((), (), s32[]{:S(2)}) async-start(), calls=%async_computation.24 | async-start | bytes 7667712 | tf_op jit(solution)/shard_map/psum | solution.py:314
  1263.1 4.9 copy-start.29
  1263.1 4.9 copy-start.52
  1263.1 4.9 copy-start.53
  1263.1 41.2 %copy-start.13 = (bf16[768,768]{1,0:T(8,128)(2,1)S(1)}, bf16[768,768]{1,0:T(8,128)(2,1)}, u32[]{:S(2)}) copy-start(bf16[768,768]{1,0:T(8,128)(2,1)} %all-gather.16.cloned.1.call-done) | copy-start | bytes 3538948
  1263.1 41.2 %copy-start.37 = (bf16[128,768]{1,0:T(8,128)(2,1)S(1)}, bf16[128,768]{1,0:T(8,128)(2,1)}, u32[]{:S(2)}) copy-start(bf16[128,768]{1,0:T(8,128)(2,1)} %reduce-scatter.25.cloned.1.call-done) | copy-start | bytes 589828
  1263.8 4.3 copy-start.55
  1263.8 4.3 copy-start.56
  1263.8 4.3 copy-start.57
  1263.8 4.3 copy-start.60
  1268.0 37.9 %copy-start.16 = (bf16[768,768]{1,0:T(8,128)(2,1)S(1)}, bf16[768,768]{1,0:T(8,128)(2,1)}, u32[]{:S(2)}) copy-start(bf16[768,768]{1,0:T(8,128)(2,1)} %all-gather.10.cloned.1.call-done) | copy-start | bytes 3538948
  (44 other events, 104.3 us)
Sparse Core Ops, SparseCore 0:
  9.6 33.6 all-gather.9
  44.9 29.5 all-gather.15
  76.1 29.5 all-gather.13
  108.0 24.8 all-gather.11
  135.1 25.6 all-gather.17
  162.3 30.4 all-gather.19
  194.3 88.6 all-gather.21
  284.5 87.8 all-gather.23
  884.8 37.9 reduce-scatter.24
  926.5 38.4 reduce-scatter.26
  967.3 29.1 reduce-scatter.28
  999.2 27.9 reduce-scatter.30
  1030.0 27.8 reduce-scatter.32
  1060.1 27.8 reduce-scatter.18
  1090.2 83.9 reduce-scatter.20
  1176.4 85.7 reduce-scatter.22
  1267.3 79.2 all-reduce.22
where the time goes:
time: 1370 us; the launch traced here: 1360 us
  local copies, waits for them, and re-layouts  761 us (56%)
  waiting for transfers between devices  415 us (30%)
  blocking collectives  64.7 us (5%)
  matrix products  55.9 us (4%)
  other arithmetic  47.3 us (3%)
  between operations  17.5 us (1%)
    gather x26, local copies, waits for them, and re-layouts, per_head_rows(): return jnp.take_along_axis(split, index.T[:, :, None], axis=0)  551 us
    unnamed x22, waiting for transfers between devices  140 us
    unnamed x193, local copies, waits for them, and re-layouts  128 us
    reduce_scatter x1, waiting for transfers between devices, body(): lax.psum_scatter(g_w_down.astype(jnp.bfloat16), 'fsdp', scatter_dimension...  88 us
    reduce_scatter x1, waiting for transfers between devices, body(): lax.psum_scatter(g_w_in.astype(jnp.bfloat16), 'fsdp', scatter_dimension=0...  86.1 us
    gather x1, local copies, waits for them, and re-layouts, body(): key_blocks = stored_blocks[order].reshape(H, groups, CLUSTER)  49.1 us
    unnamed x2, blocking collectives  39.4 us
    psum x1, waiting for transfers between devices, body(): lax.psum(shares[0].astype(jnp.bfloat16), 'ctx').astype(jnp.float32)  38.7 us
  transfers between devices with their start and end apart: 17, of which 11 were waited for; matrix products, arithmetic and copies ran while one was open for 40% of the time, Pallas kernels for 0%

commit v1 on v0

--- a/solution.py
+++ b/solution.py
@@ -8,6 +8,18 @@
 CLUSTER = 128
 EPSILON = 1e-12
 FLOOR = -1e30
+
+
+def doubled_up(value, axis, dim):
+    ways, here, step = (lax.axis_size(axis), lax.axis_index(axis), value.shape[dim])
+    line, have = (value, 1)
+    while have < ways:
+        line = jnp.concatenate(
+            [line, lax.ppermute(line, axis, [(d, (d - have) % ways) for d in range(ways)])],
+            axis=dim,
+        )
+        have = 2 * have
+    return jnp.roll(line, here * step, axis=dim)
 
 
 def layer_norm(values, gain, shift):
@@ -154,7 +166,7 @@
         shift_one,
     ) = (
         lax.all_gather(w_query, "fsdp", axis=0, tiled=True),
-        lax.all_gather(w_key, "fsdp", axis=0, tiled=True),
+        doubled_up(w_key, "fsdp", 0),
         lax.all_gather(w_value, "fsdp", axis=0, tiled=True),
         lax.all_gather(w_out, "fsdp", axis=0, tiled=True),
         lax.all_gather(b_query, "fsdp", axis=0, tiled=True),

time: 1370 us -> 1390 us (1.015)
  waiting for transfers between devices: 415 us -> 432 us
    ppermute x0 -> x2, waiting for transfers between devices: none -> 51.5 us  [doubled_up(): lax.ppermute(line, axis, [(d, (d - have) % ways) for d in range(ways)])]
    all_gather x1 -> x0, waiting for transfers between devices: 28.7 us -> none  [body(): lax.all_gather(w_key, 'fsdp', axis=0, tiled=True)]
    unnamed x193 -> x212, local copies, waits for them, and re-layouts: 128 us -> 124 us
    unnamed x22 -> x21, waiting for transfers between devices: 140 us -> 140 us
  transfers between devices with their start and end apart: 17 -> 18, of which waited for: 11 -> 11; matrix products, arithmetic and copies ran while one was open for 40% -> 39% of each run, Pallas kernels for 0% -> 0%
where the time goes in v1:
time: 1390 us; the launch traced here: 1380 us
  local copies, waits for them, and re-layouts  755 us (54%)
  waiting for transfers between devices  432 us (31%)
  blocking collectives  61.9 us (4%)
  matrix products  54.2 us (4%)
  other arithmetic  48.3 us (3%)
  between operations  17.6 us (1%)
    gather x26, local copies, waits for them, and re-layouts, per_head_rows(): return jnp.take_along_axis(split, index.T[:, :, None], axis=0)  551 us
    unnamed x21, waiting for transfers between devices  140 us
    unnamed x212, local copies, waits for them, and re-layouts  124 us
    reduce_scatter x1, waiting for transfers between devices, body(): lax.psum_scatter(g_w_in.astype(jnp.bfloat16), 'fsdp', scatter_dimension=0...  88 us
    reduce_scatter x1, waiting for transfers between devices, body(): lax.psum_scatter(g_w_down.astype(jnp.bfloat16), 'fsdp', scatter_dimension...  86.2 us
    ppermute x2, waiting for transfers between devices, doubled_up(): lax.ppermute(line, axis, [(d, (d - have) % ways) for d in range(ways)])  51.5 us
    gather x1, local copies, waits for them, and re-layouts, body(): key_blocks = stored_blocks[order].reshape(H, groups, CLUSTER)  49.1 us
    psum x1, waiting for transfers between devices, body(): lax.psum(shares[0].astype(jnp.bfloat16), 'ctx').astype(jnp.float32)  38.1 us
  transfers between devices with their start and end apart: 18, of which 11 were waited for; matrix products, arithmetic and copies ran while one was open for 39% of the time, Pallas kernels for 0%

profile of v1, /device:TPU:0, one launch (start us, length us, event | category | flops | bytes accessed | tf_op | source)
XLA Modules:
  0.0 1376.7 jit_solution(6664510178466996806)
XLA Ops:
  8.7 5.1 collective-permute-start
  13.8 6.6 collective-permute-done
  22.9 45.0 %collective-permute-done.1 = bf16[384,768]{1,0:T(8,128)(2,1)S(1)} collective-permute-done((bf16[384,768]{1,0:T(8,128)(2,1)S(1)}, bf16[384,768]{1,0:T(8,128)(2,1)S(1)}, u32[]{:S(2)}, u32[]{:S(2)}) %collective-permute-start.1) | collective-permute-done | bytes 589856 | tf_op jit(solution)/shard_map/ppermute | solution.py:18
  73.8 17.0 %all-reduce.20 = (bf16[768]{0:T(1024)(128)(2,1)S(1)}, bf16[768]{0:T(1024)(128)(2,1)S(1)}, bf16[768]{0:T(1024)(128)(2,1)S(1)}, bf16[768]{0:T(1024)(128)(2,1)S(1)}...) all-reduce(bf16[768]{0:T(1024)(128)(2,1)S(1)} %dynamic-update-slice, ...), channel_id=1, replica_groups=mesh['ctx'=8,'fsdp'=4] {'fsdp'}, use_global_device_ids=true, to_apply=%add | all-reduce | flops 5376 | bytes 21504
  95.1 3.4 reduce_window_sum.11
  99.9 45.4 %scatter_custom_fusion = s32[1536]{0:T(1024)S(1)} fusion(s32[12288]{0:T(1024)S(1)} %reshape.537, s32[12288]{0:T(1024)S(1)} %reshape.539, s32[]{:T(128)} %constant.101.clone.1), kind=kCustom, calls=%fused_computation.212 | custom fusion | bytes 6148
  147.3 4.5 gather_fusion
  151.8 5.9 gather_fusion.2
  158.4 49.1 %gather_fusion.1 = s32[12288]{0:T(1024)S(1)} fusion(s32[1024]{0:T(1024)S(1)} %gather_fusion, s32[12288]{0:T(1024)S(1)} %broadcast_clamp_fusion), kind=kCustom, calls=%fused_computation.9 | custom fusion | bytes 147456 | tf_op jit(solution)/shard_map/gather | solution.py:205
  207.6 6.2 scatter_custom_fusion.1
  214.3 14.1 %all-gather = bf16[4,1,768]{2,1,0:T(2,128)(2,1)S(1)} all-gather(bf16[1,1,768]{2,1,0:T(2,128)(2,1)S(1)} %reshape.584), channel_id=1, replica_groups=mesh['ctx'=8,'fsdp'=4] {'fsdp'}, dimensions={0}, use_global_device_ids=true | all-gather | bytes 7680 | tf_op jit(solution)/shard_map/all_gather | solution.py:181
  229.6 45.6 %scatter_custom_fusion.2 = s32[12288]{0:T(1024)S(1)} fusion(s32[12288]{0:T(1024)S(1)} %reshape.549, s32[12288]{0:T(1024)S(1)} %reshape.551, s32[]{:T(128)} %constant.101.clone.1), kind=kCustom, calls=%fused_computation.169 | custom fusion | bytes 49156
  278.5 8.5 gather_fusion.4
  288.4 3.1 copy.220
  291.5 119.4 %gather_fusion.5 = bf16[12288,64]{1,0:T(8,128)(2,1)} fusion(bf16[1024,12,64]{2,0,1:T(8,128)(2,1)S(1)} %copy.220, s32[12288]{0:T(1024)S(1)} %reshape.603), kind=kCustom, calls=%fused_computation.3.clone | custom fusion | bytes 3244032 | tf_op jit(solution)/shard_map/jit(take_along_axis)/gather | solution.py:63
  410.9 6.6 reshape.614
  423.1 119.4 %gather_fusion.3 = bf16[12288,64]{1,0:T(8,128)(2,1)} fusion(bf16[1024,12,64]{2,0,1:T(8,128)(2,1)S(1)} %copy.211, s32[12288]{0:T(1024)S(1)} %reshape.603), kind=kCustom, calls=%fused_computation.clone | custom fusion | bytes 3244032 | tf_op jit(solution)/shard_map/jit(take_along_axis)/gather | solution.py:63
  542.4 6.6 reshape.606
  549.1 10.9 broadcast_select_fusion
  565.2 8.5 gather_fusion.6
  576.6 8.6 multiply_convert_fusion
  585.3 3.6 fusion.111
  599.0 8.5 gather_fusion.7
  610.6 3.1 copy.264
  613.7 119.4 %gather_fusion.10 = bf16[12288,64]{1,0:T(8,128)(2,1)} fusion(bf16[1024,12,64]{2,0,1:T(8,128)(2,1)S(1)} %bitcast.190, s32[12288]{0:T(1024)S(1)} %reshape.627), kind=kCustom, calls=%fused_computation.7.clone | custom fusion | bytes 3244032 | tf_op jit(solution)/shard_map/jit(take_along_axis)/gather | solution.py:63
  733.0 6.6 reshape.634
  739.6 5.8 copy.251
  745.4 4.0 fusion.1
  749.4 8.4 fusion.32
  760.3 3.1 copy.262
  763.4 119.4 %gather_fusion.9 = bf16[12288,64]{1,0:T(8,128)(2,1)} fusion(bf16[1024,12,64]{2,0,1:T(8,128)(2,1)S(1)} %bitcast.189, s32[12288]{0:T(1024)S(1)} %reshape.627), kind=kCustom, calls=%fused_computation.2.clone | custom fusion | bytes 3244032 | tf_op jit(solution)/shard_map/jit(take_along_axis)/gather | solution.py:63
  882.8 6.6 reshape.630
  889.4 5.3 copy.245
  901.7 3.1 fusion.36
  904.8 8.5 gather_fusion.8
  916.2 21.9 %reduce-scatter.25.cloned.1.call-done = bf16[128,768]{1,0:T(8,128)(2,1)} async-done(((bf16[1024,768]{1,0:T(8,128)(2,1)}), bf16[128,768]{1,0:T(8,128)(2,1)}) %reduce-scatter.25.cloned.1.call-update) | async-done | bytes 196624
  941.1 39.4 %reduce-scatter.27.cloned.1.call-done = bf16[128,768]{1,0:T(8,128)(2,1)} async-done(((bf16[1024,768]{1,0:T(8,128)(2,1)}), bf16[128,768]{1,0:T(8,128)(2,1)}) %reduce-scatter.27.cloned.1.call-update) | async-done | bytes 196624
  985.3 3.6 convolution_convert_fusion
  990.1 3.7 convolution_convert_fusion.1
  993.9 18.0 %reduce-scatter.29.cloned.1.call-done = bf16[192,768]{1,0:T(8,128)(2,1)} async-done(((bf16[768,768]{1,0:T(8,128)(2,1)}), bf16[192,768]{1,0:T(8,128)(2,1)}) %reduce-scatter.29.cloned.1.call-update) | async-done | bytes 294928
  1013.8 28.4 %reduce-scatter.31.cloned.1.call-done = bf16[192,768]{1,0:T(8,128)(2,1)} async-done(((bf16[768,768]{1,0:T(8,128)(2,1)}), bf16[192,768]{1,0:T(8,128)(2,1)}) %reduce-scatter.31.cloned.1.call-update) | async-done | bytes 294928
  1044.0 28.8 %reduce-scatter.33.cloned.1.call-done = bf16[192,768]{1,0:T(8,128)(2,1)} async-done(((bf16[768,768]{1,0:T(8,128)(2,1)}), bf16[192,768]{1,0:T(8,128)(2,1)}) %reduce-scatter.33.cloned.1.call-update) | async-done | bytes 294928
  1074.7 28.4 %reduce-scatter.19.cloned.1.call-done = bf16[192,768]{1,0:T(8,128)(2,1)} async-done(((bf16[768,768]{1,0:T(8,128)(2,1)}), bf16[192,768]{1,0:T(8,128)(2,1)}) %reduce-scatter.19.cloned.1.call-update) | async-done | bytes 294928 | tf_op jit(solution)/shard_map/reduce_scatter | solution.py:288
  1103.0 86.2 %reduce-scatter.23.cloned.1.call-done = bf16[768,768]{1,0:T(8,128)(2,1)} async-done(((bf16[3072,768]{1,0:T(8,128)(2,1)}), bf16[768,768]{1,0:T(8,128)(2,1)}) %reduce-scatter.23.cloned.1.call-update) | async-done | bytes 1179664 | tf_op jit(solution)/shard_map/reduce_scatter | solution.py:312
  1189.2 88.0 %reduce-scatter.21.cloned.1.call-done = bf16[192,3072]{1,0:T(8,128)(2,1)} async-done(((bf16[768,3072]{1,0:T(8,128)(2,1)}), bf16[192,3072]{1,0:T(8,128)(2,1)}) %reduce-scatter.21.cloned.1.call-update) | async-done | bytes 1179664 | tf_op jit(solution)/shard_map/reduce_scatter | solution.py:306
  1282.8 18.8 %all-reduce.19 = (bf16[768]{0:T(1024)(128)(2,1)S(1)}, bf16[768]{0:T(1024)(128)(2,1)S(1)}, bf16[768]{0:T(1024)(128)(2,1)S(1)}, bf16[768]{0:T(1024)(128)(2,1)S(1)}...) all-reduce(bf16[768]{0:T(1024)(128)(2,1)} %copy-done.56, ...), channel_id=1, replica_groups=mesh['ctx'=8,'fsdp'=4] {'fsdp'}, use_global_device_ids=true, to_apply=%add.7 | all-reduce | flops 9984 | bytes 39936
  1302.3 12.0 all-reduce.17
  1323.5 38.1 %all-reduce.23.cloned.1.call-done = (bf16[192,768]{0,1:T(8,128)(2,1)}, bf16[192,768]{0,1:T(8,128)(2,1)}, bf16[192,768]{0,1:T(8,128)(2,1)}, bf16[192,768]{1,0:T(8...) async-done(((bf16[192,768]{0,1:T(8,128)(2,1)}, bf16[192,768]{0,1:T(8,128)(2,1)}, bf16[192,768]{0,1:T(8,128)(2,1)}, bf16[192,768]{1,0:T(8,128)(2,1)}, ...) | async-done | bytes 3538960 | tf_op jit(solution)/shard_map/psum | solution.py:326
  (378 shorter events, 99.6 us)
Async XLA Ops:
  7.2 140.1 %copy-start = (s32[1,1024]{1,0:T(1,128)S(1)}, s32[1,1024]{1,0:T(1,128)}, u32[]{:S(2)}) copy-start(s32[1,1024]{1,0:T(1,128)} %param.27) | copy-start | bytes 12292
  7.2 15.7 %copy-start.23 = (bf16[192,768]{1,0:T(8,128)(2,1)S(1)}, bf16[192,768]{1,0:T(8,128)(2,1)}, u32[]{:S(2)}) copy-start(bf16[192,768]{1,0:T(8,128)(2,1)} %param.30) | copy-start | bytes 884740
  7.2 83.5 %all-gather.9.cloned.1.call-start = ((), (), s32[]{:S(2)}) async-start(), calls=%async_computation.8 | async-start | bytes 1474560 | tf_op jit(solution)/shard_map/all_gather | solution.py:170
  7.9 268.5 %all-gather.13.cloned.1.call-start = ((), (), s32[]{:S(2)}) async-start(), calls=%async_computation.10 | async-start | bytes 1474560 | tf_op jit(solution)/shard_map/all_gather | solution.py:168
  8.7 279.7 %all-gather.15.cloned.1.call-start = ((), (), s32[]{:S(2)}) async-start(), calls=%async_computation.11 | async-start | bytes 1769472 | tf_op jit(solution)/shard_map/all_gather | solution.py:201
  8.7 11.7 collective-permute-start
  21.4 46.5 %collective-permute-start.1 = (bf16[384,768]{1,0:T(8,128)(2,1)S(1)}, bf16[384,768]{1,0:T(8,128)(2,1)S(1)}, u32[]{:S(2)}, u32[]{:S(2)}) collective-permute-start(bf16[384,768]{1,0:T(8,128)(2,1)S(1)} %pad_maximum_fusion), channel_id=1, source_target_pairs={{0,2},{1,3},{2,0},{3,1},{4,6},{5,7},{6,4},{7,5},{8,10},{9,11},{10,... | collective-permute-start | bytes 1769480 | tf_op jit(solution)/shard_map/ppermute | solution.py:18
  22.9 46.6 %copy-start.8 = (bf16[1,128,768]{2,1,0:T(8,128)(2,1)S(1)}, bf16[1,128,768]{2,1,0:T(8,128)(2,1)}, u32[]{:S(2)}) copy-start(bf16[1,128,768]{2,1,0:T(8,128)(2,1)} %param.25) | copy-start | bytes 589828
  68.0 4.8 copy-start.71
  68.1 5.0 copy-start.72
  68.1 5.2 copy-start.73
  68.1 5.4 copy-start.74
  70.8 346.7 %all-gather.11.cloned.1.call-start = ((), (), s32[]{:S(2)}) async-start(), calls=%async_computation.9 | async-start | bytes 1769472 | tf_op jit(solution)/shard_map/all_gather | solution.py:202
  93.1 5.8 copy-start.61
  93.1 5.8 copy-start.67
  93.1 481.5 %all-gather.17.cloned.1.call-start = ((), (), s32[]{:S(2)}) async-start(), calls=%async_computation.12 | async-start | bytes 1474560 | tf_op jit(solution)/shard_map/all_gather | solution.py:171
  93.7 5.6 copy-start.62
  93.7 5.6 copy-start.66
  93.7 482.9 %all-gather.19.cloned.1.call-start = ((), (), s32[]{:S(2)}) async-start(), calls=%async_computation.13 | async-start | bytes 5898240 | tf_op jit(solution)/shard_map/all_gather | solution.py:179
  94.3 491.0 %all-gather.21.cloned.1.call-start = ((), (), s32[]{:S(2)}) async-start(), calls=%async_computation.14 | async-start | bytes 5898240 | tf_op jit(solution)/shard_map/all_gather | solution.py:180
  95.0 843.1 %reduce-scatter.25.cloned.1.call-start = ((), (), s32[]{:S(2)}) async-start(), calls=%async_computation.18 | async-start | bytes 1769472
  158.4 55.9 %copy-start.64 = (bf16[768]{0:T(1024)(128)(2,1)S(1)}, bf16[768]{0:T(1024)(128)(2,1)}, u32[]{:S(2)}) copy-start(bf16[768]{0:T(1024)(128)(2,1)} %param.39) | copy-start | bytes 4612
  542.4 6.6 copy-start.41
  549.1 11.0 copy-start.31
  549.1 11.0 copy-start.37
  560.0 5.1 copy-start.3
  576.4 20.3 %copy-start.4 = (f32[128,768]{1,0:T(8,128)}, f32[128,768]{1,0:T(8,128)S(1)}, u32[]{:S(2)}) copy-start(f32[128,768]{1,0:T(8,128)S(1)} %get-tuple-element.175) | copy-start | bytes 1179652
  576.6 20.1 %copy-start.50 = (f32[128]{0:T(128)}, f32[128]{0:T(128)S(1)}, u32[]{:S(2)}) copy-start(f32[128]{0:T(128)S(1)} %fusion.97) | copy-start | bytes 1540
  576.6 8.6 copy-start.49
  585.3 5.6 slice-start.2
  585.3 5.6 slice-start.3
  585.3 5.6 copy-start.77
  739.6 5.8 copy-start.32
  749.4 9.1 copy-start.17
  889.4 5.3 copy-start.48
  899.0 81.5 %reduce-scatter.27.cloned.1.call-start = ((), (), s32[]{:S(2)}) async-start(), calls=%async_computation.19 | async-start | bytes 1769472
  900.7 111.2 %reduce-scatter.29.cloned.1.call-start = ((), (), s32[]{:S(2)}) async-start(), calls=%async_computation.20 | async-start | bytes 1474560
  916.2 125.9 %reduce-scatter.31.cloned.1.call-start = ((), (), s32[]{:S(2)}) async-start(), calls=%async_computation.21 | async-start | bytes 1474560
  941.0 131.7 %reduce-scatter.33.cloned.1.call-start = ((), (), s32[]{:S(2)}) async-start(), calls=%async_computation.22 | async-start | bytes 1474560
  983.5 119.6 %reduce-scatter.19.cloned.1.call-start = ((), (), s32[]{:S(2)}) async-start(), calls=%async_computation.15 | async-start | bytes 1474560 | tf_op jit(solution)/shard_map/reduce_scatter | solution.py:288
  985.1 204.2 %reduce-scatter.23.cloned.1.call-start = ((), (), s32[]{:S(2)}) async-start(), calls=%async_computation.17 | async-start | bytes 5898240 | tf_op jit(solution)/shard_map/reduce_scatter | solution.py:312
  988.9 288.3 %reduce-scatter.21.cloned.1.call-start = ((), (), s32[]{:S(2)}) async-start(), calls=%async_computation.16 | async-start | bytes 5898240 | tf_op jit(solution)/shard_map/reduce_scatter | solution.py:306
  993.8 367.8 %all-reduce.23.cloned.1.call-start = ((), (), s32[]{:S(2)}) async-start(), calls=%async_computation.23 | async-start | bytes 7667712 | tf_op jit(solution)/shard_map/psum | solution.py:326
  1278.1 4.7 copy-start.53
  1278.1 4.7 copy-start.54
  1278.1 4.7 copy-start.55
  1278.1 41.4 %copy-start.13 = (bf16[768,768]{1,0:T(8,128)(2,1)S(1)}, bf16[768,768]{1,0:T(8,128)(2,1)}, u32[]{:S(2)}) copy-start(bf16[768,768]{1,0:T(8,128)(2,1)} %all-gather.9.cloned.1.call-done) | copy-start | bytes 3538948
  1282.7 37.3 %copy-start.38 = (bf16[128,768]{1,0:T(8,128)(2,1)S(1)}, bf16[128,768]{1,0:T(8,128)(2,1)}, u32[]{:S(2)}) copy-start(bf16[128,768]{1,0:T(8,128)(2,1)} %reduce-scatter.25.cloned.1.call-done) | copy-start | bytes 589828
  (52 other events, 126.5 us)
Sparse Core Ops, SparseCore 0:
  9.6 55.0 all-gather.8
  66.3 29.0 all-gather.12
  97.9 25.0 all-gather.14
  125.3 25.6 all-gather.10
  152.4 30.4 all-gather.16
  184.3 88.6 all-gather.18
  274.6 87.8 all-gather.20
  899.2 38.9 reduce-scatter.24
  942.0 38.4 reduce-scatter.26
  982.7 29.1 reduce-scatter.28
  1014.2 27.8 reduce-scatter.30
  1044.9 27.8 reduce-scatter.32
  1075.1 27.8 reduce-scatter.18
  1105.2 83.9 reduce-scatter.22
  1191.4 85.7 reduce-scatter.20
  1282.3 79.2 all-reduce.22
